TPU v7x, 256 devices: a whole 4x4x8 slice. The times are simulated.
256 devices in a mesh: fsdp: 32 (over z, y), tp: 8 (over x, core).
Axes of the slice: x: 4, y: 4, z: 8, core: 2. Of those that a mesh axis runs over, the one named last changes fastest.
Arguments:
- tokens: bfloat16 [8192, 4096], P('fsdp', 'tp'), may hold values from -6 to 6
- cotangent: bfloat16 [8192, 4096], P('fsdp', 'tp'), may hold values from -6 to 6
- up_weight: bfloat16 [4096, 14336], P('fsdp', 'tp'), may hold values from -0.1875 to 0.1875
- down_weight: bfloat16 [4096, 14336], P('fsdp', 'tp'), may hold values from -0.09375 to 0.09375
- up_list: int32 [8, 128, 2], P('tp'), may hold values from 0 to 31, as said below
- up_count: int32 [8], P('tp'), may hold values from 35 to 128, as said below
- down_list: int32 [8, 128, 2], P('tp'), may hold values from 0 to 31, as said below
- down_count: int32 [8], P('tp'), may hold values from 35 to 128, as said below
Outputs:
- mixed: bfloat16 [8192, 4096], P('fsdp', 'tp')
- grad_tokens: bfloat16 [8192, 4096], P('fsdp', 'tp')
- grad_up: float32 [4096, 14336], P('fsdp', 'tp')
- grad_down: float32 [4096, 14336], P('fsdp', 'tp')
Inputs may be any that keep to these rules, and one draw needn't show every extreme that they name: `up_list`: in each slice's list the first count entries are distinct pairs (row block below 32, column block below 14), in no particular order; every row block has at least one and at most 4 of them; in every slice the one row block held by some index of fsdp have exactly 4, and in some slice every row block has exactly 4. Entries from the count on are arbitrary pairs in range and carry no meaning. `up_count`: the number of valid entries of each slice's up list. `down_list`: as for up_list. `down_count`: the number of valid entries of each slice's down list.
All inputs are finite; a program needn't handle non-finite values.
Results may differ from a plain program's by a relative error of at most 0.015.
Values may be sent and summed in bfloat16 or wider, within the bound.
No kernel may reach another device: no remote copies, remote signals or barrier semaphores. Data moves between devices by JAX's collectives and lax.ppermute only.
A program may use at most 256 MiB of HBM per device.

v0:
```python
import jax
import jax.numpy as jnp
from jax import lax
from jax.sharding import PartitionSpec as P

BLK = 128
SQRT_TWO_PI = 0.7978845608028654
CUBIC = 0.044715


def gelu_tanh(values):
    inner = SQRT_TWO_PI * (values + CUBIC * values * values * values)
    return 0.5 * values * (1.0 + jnp.tanh(inner))


def gelu_slope(values):
    tangent = jnp.tanh(SQRT_TWO_PI * (values + CUBIC * values * values * values))
    return 0.5 * (1.0 + tangent) + 0.5 * values * (1.0 - tangent * tangent) * SQRT_TWO_PI * (
        1.0 + 3.0 * CUBIC * values * values
    )


def list_table(entries, number):
    valid = jnp.arange(entries.shape[0], dtype=jnp.int32) < number
    return (entries[:, 0], entries[:, 1], valid)


def slot_table(entries, number, owner_blocks, owners, capacity):
    rows, cols, valid = list_table(entries, number)
    owner = rows // owner_blocks
    member = (
        (owner[:, None] == jnp.arange(owners, dtype=jnp.int32)[None, :]) & valid[:, None]
    ).astype(jnp.int32)
    earlier = jnp.cumsum(member, axis=0) - member
    rank = jnp.sum(earlier * member, axis=1)
    slot = owner * capacity + rank
    chosen = (
        valid[:, None] & (slot[:, None] == jnp.arange(owners * capacity, dtype=jnp.int32)[None, :])
    ).astype(jnp.int32)
    slot_rows = jnp.sum(chosen * rows[:, None], axis=0)
    slot_cols = jnp.sum(chosen * cols[:, None], axis=0)
    slot_valid = jnp.sum(chosen, axis=0) > 0
    return (slot_rows, slot_cols, slot_valid)


def pick_blocks(weight, table, row_offset):
    rows, cols, valid = table
    row_count = weight.shape[0] // BLK
    col_count = weight.shape[1] // BLK
    tiles = weight.reshape(row_count, BLK, col_count, BLK)
    local_rows = jnp.clip(rows - row_offset, 0, row_count - 1)
    picked = tiles[local_rows, :, cols, :]
    return jnp.where(valid[:, None, None], picked, jnp.zeros((), weight.dtype))


def place_grads(tiles, table, first_block, block_count, col_blocks):
    rows, cols, valid = table
    inside = valid & (rows >= first_block) & (rows < first_block + block_count)
    local_rows = jnp.clip(rows - first_block, 0, block_count - 1)
    kept = jnp.where(inside[:, None, None], tiles, jnp.zeros((), jnp.float32))
    spread = (
        jnp.zeros((block_count, BLK, col_blocks, BLK), jnp.float32)
        .at[local_rows, :, cols, :]
        .add(kept)
    )
    return spread.reshape(block_count * BLK, col_blocks * BLK)


def fetch(up_weight, down_weight, up_table, down_table, capacity, owner_blocks):
    first_slot = lax.axis_index("fsdp") * capacity
    up_mine = tuple((lax.dynamic_slice_in_dim(member, first_slot, capacity) for member in up_table))
    down_mine = tuple(
        (lax.dynamic_slice_in_dim(member, first_slot, capacity) for member in down_table)
    )
    offset = lax.axis_index("fsdp") * owner_blocks
    return (
        lax.all_gather(pick_blocks(up_weight, up_mine, offset), "fsdp", axis=0, tiled=True),
        lax.all_gather(pick_blocks(down_weight, down_mine, offset), "fsdp", axis=0, tiled=True),
    )


def body(tokens, cotangent, up_weight, down_weight, up_list, up_count, down_list, down_count):
    owner_blocks = up_weight.shape[0] // BLK
    col_blocks = up_weight.shape[1] // BLK
    owners = lax.axis_size("fsdp")
    group_rows = tokens.shape[0]
    up_table = slot_table(
        up_list[0],
        up_count[0],
        owner_blocks,
        owners,
        owner_blocks * (up_list.shape[1] // (owners * owner_blocks)),
    )
    down_table = slot_table(
        down_list[0],
        down_count[0],
        owner_blocks,
        owners,
        owner_blocks * (down_list.shape[1] // (owners * owner_blocks)),
    )
    capacity = up_list.shape[1] // owners
    up_blocks, down_blocks = fetch(
        up_weight, down_weight, up_table, down_table, capacity, owner_blocks
    )
    gathered = lax.all_gather(tokens, "tp", axis=1, tiled=True)
    width = gathered.shape[1]
    row_blocks = width // BLK
    x_tiles = gathered.reshape(group_rows, row_blocks, BLK)
    x_taken = jnp.take(x_tiles, up_table[0], axis=1)
    partial_up = jnp.einsum("rsk,skn->rsn", x_taken, up_blocks, preferred_element_type=jnp.float32)
    hidden = (
        jnp.zeros((group_rows, col_blocks, BLK), jnp.float32).at[:, up_table[1], :].add(partial_up)
    )
    active = gelu_tanh(hidden).astype(jnp.bfloat16)
    active_taken = jnp.take(active, down_table[1], axis=1)
    layer_product = jnp.einsum(
        "rsn,skn->rsk", active_taken, down_blocks, preferred_element_type=jnp.float32
    )
    layer_parts = (
        jnp.zeros((group_rows, row_blocks, BLK), jnp.float32)
        .at[:, down_table[0], :]
        .add(layer_product)
    )
    mixed = lax.psum_scatter(
        layer_parts.reshape(group_rows, width).astype(jnp.bfloat16),
        "tp",
        scatter_dimension=1,
        tiled=True,
    )
    up_again, down_again = fetch(
        up_weight, down_weight, up_table, down_table, capacity, owner_blocks
    )
    grad_in = lax.all_gather(cotangent, "tp", axis=1, tiled=True)
    dy_tiles = grad_in.reshape(group_rows, row_blocks, BLK)
    dy_taken = jnp.take(dy_tiles, down_table[0], axis=1)
    back_down = jnp.einsum("rsk,skn->rsn", dy_taken, down_again, preferred_element_type=jnp.float32)
    grad_active = (
        jnp.zeros((group_rows, col_blocks, BLK), jnp.float32).at[:, down_table[1], :].add(back_down)
    )
    grad_hidden = (grad_active * gelu_slope(hidden)).astype(jnp.bfloat16)
    hidden_taken = jnp.take(grad_hidden, up_table[1], axis=1)
    back_up = jnp.einsum("rsn,skn->rsk", hidden_taken, up_again, preferred_element_type=jnp.float32)
    input_parts = (
        jnp.zeros((group_rows, row_blocks, BLK), jnp.float32).at[:, up_table[0], :].add(back_up)
    )
    grad_tokens = lax.psum_scatter(
        input_parts.reshape(group_rows, width).astype(jnp.bfloat16),
        "tp",
        scatter_dimension=1,
        tiled=True,
    )
    up_rows_part = up_table[0]
    up_cols_part = up_table[1]
    down_rows_part = down_table[0]
    down_cols_part = down_table[1]
    x_part = jnp.take(x_tiles, up_rows_part, axis=1)
    hidden_part = jnp.take(grad_hidden, up_cols_part, axis=1)
    dy_part = jnp.take(dy_tiles, down_rows_part, axis=1)
    active_part = jnp.take(active, down_cols_part, axis=1)
    up_term = jnp.einsum("rsk,rsn->skn", x_part, hidden_part, preferred_element_type=jnp.float32)
    down_term = jnp.einsum("rsk,rsn->skn", dy_part, active_part, preferred_element_type=jnp.float32)
    summed = lax.psum_scatter(
        jnp.stack([up_term, down_term], axis=1).astype(jnp.bfloat16),
        "fsdp",
        scatter_dimension=0,
        tiled=True,
    ).astype(jnp.float32)
    first_slot = lax.axis_index("fsdp") * capacity
    offset = lax.axis_index("fsdp") * owner_blocks
    up_mine = tuple((lax.dynamic_slice_in_dim(member, first_slot, capacity) for member in up_table))
    down_mine = tuple(
        (lax.dynamic_slice_in_dim(member, first_slot, capacity) for member in down_table)
    )
    grad_up = place_grads(summed[:, 0], up_mine, offset, owner_blocks, col_blocks)
    grad_down = place_grads(summed[:, 1], down_mine, offset, owner_blocks, col_blocks)
    return (mixed, grad_tokens, grad_up, grad_down)


def solution(mesh):
    return jax.shard_map(
        body,
        mesh=mesh,
        in_specs=(
            P("fsdp", "tp"),
            P("fsdp", "tp"),
            P("fsdp", "tp"),
            P("fsdp", "tp"),
            P("tp", None, None),
            P("tp"),
            P("tp", None, None),
            P("tp"),
        ),
        out_specs=(P("fsdp", "tp"), P("fsdp", "tp"), P("fsdp", "tp"), P("fsdp", "tp")),
        check_vma=False,
    )
```

profile of v0, /device:TPU:1, one launch (start us, length us, event | category | flops | bytes accessed | tf_op | source)
XLA Modules:
  0.0 681.6 jit_solution(12440131534698281654)
XLA Ops:
  24.6 17.8 %all-gather.9.cloned.1.call-done = bf16[256,4096]{0,1:T(8,128)(2,1)} async-done(((bf16[256,512]{0,1:T(8,128)(2,1)}), bf16[256,4096]{0,1:T(8,128)(2,1)}) %all-gather.9.cloned.1.call-update) | async-done | bytes 2097168 | tf_op jit(solution)/shard_map/all_gather | solution.py:105
  42.5 3.2 copy.65
  45.7 27.4 %all-gather.11.cloned.1.call-done = bf16[256,4096]{0,1:T(8,128)(2,1)} async-done(((bf16[256,512]{0,1:T(8,128)(2,1)}), bf16[256,4096]{0,1:T(8,128)(2,1)}) %all-gather.11.cloned.1.call-update) | async-done | bytes 2097168 | tf_op jit(solution)/shard_map/all_gather | solution.py:133
  73.1 4.1 copy.72
  77.2 6.5 gather_fusion.2
  83.7 8.1 %gather_fusion.4 = bf16[128,256,128]{2,1,0:T(8,128)(2,1)} fusion(bf16[256,32,128]{2,0,1:T(8,128)(2,1)} %copy.72, s32[1024]{0:T(1024)S(1)} %pad_clamp_fusion.1), kind=kCustom, calls=%fused_computation.2.clone | custom fusion | bytes 16777728 | tf_op jit(solution)/shard_map/jit(_take)/gather | solution.py:135
  91.8 62.8 %all-gather.7.cloned.1.call-done = bf16[128,128,128]{2,1,0:T(8,128)(2,1)} async-done(((bf16[4,128,128]{2,1,0:T(8,128)(2,1)}), bf16[128,128,128]{2,1,0:T(8,128)(2,1)}) %all-gather.7.cloned.1.call-update) | async-done | bytes 4194320 | tf_op jit(solution)/shard_map/all_gather | solution.py:77
  154.6 12.7 %fusion.12 = f32[128,256,128]{2,1,0:T(8,128)} fusion(bf16[128,128,128]{2,1,0:T(8,128)(2,1)} %all-gather.7.cloned.1.call-done, bf16[128,256,128]{2,1,0:T(8,128)(2,1)} %gather_fusion.2, pred[128]{0:T(512)(128)(4,1)S(1)} %get-tuple-element.49), kind=kOutput, calls=%fused_computation.25 | convolution fusion | flops 1077936128 | bytes 29360256 | tf_op jit(solution)/shard_map/rsk,skn->rsn/dot_general | solution.py:110
  167.4 24.3 %scatter_fusion = f32[256,14,128]{2,0,1:T(8,128)S(1)} fusion(f32[256,14,128]{2,0,1:T(8,128)S(1)} %broadcast.166.clone.1, s32[128]{0:T(128)S(1)} %fusion.38, f32[128,256,128]{2,1,0:T(8,128)} %fusion.12), kind=kCustom, calls=%fused_computation.6 | custom fusion | flops 4194304 | bytes 50332160 | tf_op jit(solution)/shard_map/scatter-add | solution.py:112
  191.7 44.5 %all-gather.5.cloned.1.call-done = bf16[128,128,128]{2,1,0:T(8,128)(2,1)} async-done(((bf16[4,128,128]{2,1,0:T(8,128)(2,1)}), bf16[128,128,128]{2,1,0:T(8,128)(2,1)}) %all-gather.5.cloned.1.call-update) | async-done | bytes 4194320 | tf_op jit(solution)/shard_map/all_gather | solution.py:78
  236.2 12.7 %fusion.6 = f32[128,256,128]{2,1,0:T(8,128)} fusion(bf16[128,128,128]{2,1,0:T(8,128)(2,1)} %all-gather.5.cloned.1.call-done, bf16[128,256,128]{2,1,0:T(8,128)(2,1)} %gather_fusion.4, pred[128]{0:T(512)(128)(4,1)S(1)} %get-tuple-element.44), kind=kOutput, calls=%fused_computation.19 | convolution fusion | flops 1077936128 | bytes 29360256 | tf_op jit(solution)/shard_map/rsk,skn->rsn/dot_general | solution.py:136
  250.4 36.6 %scatter_fusion.2 = f32[256,14,128]{2,0,1:T(8,128)} fusion(f32[256,14,128]{2,0,1:T(8,128)} %broadcast.166.clone, s32[128]{0:T(128)S(1)} %fusion.40, f32[128,256,128]{2,1,0:T(8,128)} %fusion.6), kind=kCustom, calls=%fused_computation.8 | custom fusion | flops 4194304 | bytes 50332160 | tf_op jit(solution)/shard_map/scatter-add | solution.py:138
  287.0 3.7 fusion.28
  290.7 7.7 %gather_fusion.5 = bf16[128,256,128]{2,1,0:T(8,128)(2,1)} fusion(bf16[256,14,128]{2,0,1:T(8,128)(2,1)} %get-tuple-element.36, s32[1024]{0:T(1024)S(1)} %pad_clamp_fusion), kind=kCustom, calls=%fused_computation.3.clone | custom fusion | bytes 16777728 | tf_op jit(solution)/shard_map/jit(_take)/gather | solution.py:141
  298.4 12.7 %fusion.2 = f32[128,256,128]{2,1,0:T(8,128)} fusion(bf16[128,128,128]{2,1,0:T(8,128)(2,1)} %all-gather.7.cloned.1.call-done, bf16[128,256,128]{2,1,0:T(8,128)(2,1)} %gather_fusion.5, pred[128]{0:T(512)(128)(4,1)S(1)} %get-tuple-element.48), kind=kOutput, calls=%fused_computation.15 | convolution fusion | flops 1077936128 | bytes 29360256 | tf_op jit(solution)/shard_map/rsn,skn->rsk/dot_general | solution.py:142
  313.5 35.7 %scatter_fusion.3 = f32[256,32,128]{2,0,1:T(8,128)} fusion(f32[256,32,128]{2,0,1:T(8,128)} %broadcast.160.clone.1, s32[128]{0:T(128)S(1)} %fusion.39, f32[128,256,128]{2,1,0:T(8,128)} %fusion.2), kind=kCustom, calls=%fused_computation.9 | custom fusion | flops 4194304 | bytes 50332160 | tf_op jit(solution)/shard_map/scatter-add | solution.py:144
  354.6 6.7 gather_fusion.3
  361.4 12.7 %fusion.9 = f32[128,256,128]{2,1,0:T(8,128)} fusion(bf16[128,128,128]{2,1,0:T(8,128)(2,1)} %all-gather.5.cloned.1.call-done, bf16[128,256,128]{2,1,0:T(8,128)(2,1)} %gather_fusion.3, pred[128]{0:T(512)(128)(4,1)S(1)} %get-tuple-element.45), kind=kOutput, calls=%fused_computation.22 | convolution fusion | flops 1077936128 | bytes 29360256 | tf_op jit(solution)/shard_map/rsn,skn->rsk/dot_general | solution.py:116
  376.6 35.8 %scatter_fusion.1 = f32[256,32,128]{2,0,1:T(8,128)} fusion(f32[256,32,128]{2,0,1:T(8,128)} %broadcast.160.clone, s32[128]{0:T(128)S(1)} %fusion.37, f32[128,256,128]{2,1,0:T(8,128)} %fusion.9), kind=kCustom, calls=%fused_computation.7 | custom fusion | flops 4194304 | bytes 50332160 | tf_op jit(solution)/shard_map/scatter-add | solution.py:122
  417.9 8.1 %convert_bitcast_fusion = bf16[128,1,128,128]{3,2,0,1:T(8,128)(2,1)S(1)} fusion(bf16[128,256,128]{2,1,0:T(8,128)(2,1)} %gather_fusion.3, pred[128]{0:T(512)(128)(4,1)S(1)} %get-tuple-element.45, bf16[128,256,128]{2,1,0:T(8,128)(2,1)} %gather_fusion.4, pred[128]{0:T(512)(128)(4,1)S(1)} %get-tuple-element.44), kind=kOutput, calls=%fused_computation.31 | convolution fusion | flops 1084227584 | bytes 20971776 | tf_op jit(solution)/shard_map/rsk,rsn->skn/dot_general | solution.py:161
  426.0 9.3 %convert_bitcast_fusion.1 = bf16[128,1,128,128]{3,2,0,1:T(8,128)(2,1)} fusion(bf16[128,256,128]{2,1,0:T(8,128)(2,1)} %gather_fusion.5, pred[128]{0:T(512)(128)(4,1)S(1)} %get-tuple-element.48, bf16[128,256,128]{2,1,0:T(8,128)(2,1)} %gather_fusion.2, pred[128]{0:T(512)(128)(4,1)S(1)} %get-tuple-element.49), kind=kOutput, calls=%fused_computation.32 | convolution fusion | flops 1084227584 | bytes 20971776 | tf_op jit(solution)/shard_map/rsk,rsn->skn/dot_general | solution.py:160
  435.2 6.3 pad_maximum_fusion
  445.2 7.0 %reduce-scatter.6.cloned.1.call-done = bf16[256,512]{0,1:T(8,128)(2,1)} async-done(((bf16[256,4096]{0,1:T(8,128)(2,1)}), bf16[256,512]{0,1:T(8,128)(2,1)}) %reduce-scatter.6.cloned.1.call-update) | async-done | bytes 262160 | tf_op jit(solution)/shard_map/reduce_scatter | solution.py:124
  454.0 214.8 %all-reduce.3.cloned.1.call-done = bf16[128,2,128,128]{3,2,0,1:T(8,128)(2,1)} async-done(((bf16[128,2,128,128]{3,2,0,1:T(8,128)(2,1)}), bf16[128,2,128,128]{3,2,0,1:T(8,128)(2,1)}) %all-reduce.3.cloned.1.call-update) | async-done | bytes 8388624
  (91 shorter events, 44.1 us)
Async XLA Ops:
  7.2 35.3 %all-gather.9.cloned.1.call-start = ((), (), s32[]{:S(2)}) async-start(), calls=%async_computation.4 | async-start | bytes 2359296 | tf_op jit(solution)/shard_map/all_gather | solution.py:105
  9.0 64.1 %all-gather.11.cloned.1.call-start = ((), (), s32[]{:S(2)}) async-start(), calls=%async_computation.6 | async-start | bytes 2359296 | tf_op jit(solution)/shard_map/all_gather | solution.py:133
  10.9 143.7 %all-gather.7.cloned.1.call-start = ((), (), s32[]{:S(2)}) async-start(), calls=%async_computation.3 | async-start | bytes 4325376 | tf_op jit(solution)/shard_map/all_gather | solution.py:77
  20.6 215.6 %all-gather.5.cloned.1.call-start = ((), (), s32[]{:S(2)}) async-start(), calls=%async_computation.2 | async-start | bytes 4325376 | tf_op jit(solution)/shard_map/all_gather | solution.py:78
  24.3 419.2 %reduce-scatter.8.cloned.1.call-start = ((), (), s32[]{:S(2)}) async-start(), calls=%async_computation.7 | async-start | bytes 2359296 | tf_op jit(solution)/shard_map/reduce_scatter | solution.py:146
  354.6 97.7 %reduce-scatter.6.cloned.1.call-start = ((), (), s32[]{:S(2)}) async-start(), calls=%async_computation.5 | async-start | bytes 2359296 | tf_op jit(solution)/shard_map/reduce_scatter | solution.py:124
  417.8 251.0 %all-reduce.3.cloned.1.call-start = ((), (), s32[]{:S(2)}) async-start(), calls=%async_computation.8 | async-start | bytes 16777216
  441.5 0.7 copy-start.4
  441.5 228.3 %copy-start = (pred[4]{0:T(512)(128)(4,1)S(1)}, pred[4]{0:T(512)(128)(4,1)}, u32[]{:S(2)}) copy-start(pred[4]{0:T(512)(128)(4,1)} %get-tuple-element.32) | copy-start | bytes 16
  441.5 228.3 %copy-start.1 = (pred[4]{0:T(512)(128)(4,1)S(1)}, pred[4]{0:T(512)(128)(4,1)}, u32[]{:S(2)}) copy-start(pred[4]{0:T(512)(128)(4,1)} %get-tuple-element.28) | copy-start | bytes 16
  441.5 228.5 %copy-start.3 = (s32[4]{0:T(128)S(1)}, s32[4]{0:T(128)}, u32[]{:S(2)}) copy-start(s32[4]{0:T(128)} %get-tuple-element.30) | copy-start | bytes 52
  441.5 230.9 %copy-start.2 = (s32[4]{0:T(128)S(1)}, s32[4]{0:T(128)}, u32[]{:S(2)}) copy-start(s32[4]{0:T(128)} %get-tuple-element.46) | copy-start | bytes 52
Sparse Core Ops, SparseCore 0:
  10.4 32.0 all-gather.8
  44.9 28.1 all-gather.10
  76.2 78.3 all-gather.6
  157.6 78.5 all-gather.4
  354.7 34.2 reduce-scatter.7
  417.9 34.2 reduce-scatter.5
  455.9 212.8 all-reduce.2
where the time goes:
time: 683 us; the launch traced here: 682 us
  waiting for transfers between devices  375 us (55%)
  other arithmetic  156 us (23%)
  matrix products  68.1 us (10%)
  local copies, waits for them, and re-layouts  66 us (10%)
  between operations  16.4 us (2%)
    unnamed x8, waiting for transfers between devices  215 us
    all_gather x1, waiting for transfers between devices, fetch(): lax.all_gather(pick_blocks(up_weight, up_mine, offset), 'fsdp', axis=0, t...  62.8 us
    all_gather x1, waiting for transfers between devices, fetch(): lax.all_gather(pick_blocks(down_weight, down_mine, offset), 'fsdp', axis=...  44.5 us
    scatter-add x1, other arithmetic, body(): jnp.zeros((group_rows, col_blocks, BLK), jnp.float32)  36.6 us
    scatter-add x1, other arithmetic, body(): layer_parts = jnp.zeros((group_rows, row_blocks, BLK), jnp.float32).at[:,...  35.8 us
    scatter-add x1, other arithmetic, body(): jnp.zeros((group_rows, row_blocks, BLK), jnp.float32).at[:, up_table[0], :]  35.7 us
    all_gather x1, waiting for transfers between devices, body(): grad_in = lax.all_gather(cotangent, 'tp', axis=1, tiled=True)  27.4 us
    scatter-add x1, other arithmetic, body(): jnp.zeros((group_rows, col_blocks, BLK), jnp.float32).at[:, up_table[1], :]  24.3 us
  transfers between devices with their start and end apart: 7, of which 6 were waited for; matrix products, arithmetic and copies ran while one was open for 24% of the time, Pallas kernels for 0%

commit v1 on v0

--- a/solution.py
+++ b/solution.py
@@ -75,7 +75,15 @@
     offset = lax.axis_index("fsdp") * owner_blocks
     return (
         lax.all_gather(pick_blocks(up_weight, up_mine, offset), "fsdp", axis=0, tiled=True),
-        lax.all_gather(pick_blocks(down_weight, down_mine, offset), "fsdp", axis=0, tiled=True),
+        jnp.concatenate(
+            lax.all_to_all(
+                jnp.stack([pick_blocks(down_weight, down_mine, offset)] * lax.axis_size("fsdp")),
+                "fsdp",
+                0,
+                0,
+            ),
+            axis=0,
+        ),
     )
 
 

time: 683 us -> 617 us (0.903)
  waiting for transfers between devices: 375 us -> 295 us
  starting transfers between devices: 0.47 us -> 12.6 us
    all_gather x1, waiting for transfers between devices: 62.8 us -> 0.02 us  [fetch(): lax.all_gather(pick_blocks(up_weight, up_mine, offset), 'fsdp', axis=0, t...]
    all_gather x1 -> x0, waiting for transfers between devices: 44.5 us -> none  [fetch(): lax.all_gather(pick_blocks(down_weight, down_mine, offset), 'fsdp', axis=...]
    all_to_all x0 -> x1, waiting for transfers between devices: none -> 40.8 us  [fetch(): lax.all_to_all(jnp.stack([pick_blocks(down_weight, down_mine, offset)] *...]
    all_gather x1, waiting for transfers between devices: 27.4 us -> 4.36 us  [body(): grad_in = lax.all_gather(cotangent, 'tp', axis=1, tiled=True)]
    scatter-add x1, other arithmetic: 24.3 us -> 36.7 us  [body(): jnp.zeros((group_rows, col_blocks, BLK), jnp.float32).at[:, up_table[1], :]]
    scatter-add x1, other arithmetic: 36.6 us -> 24.4 us  [body(): jnp.zeros((group_rows, col_blocks, BLK), jnp.float32)]
    all_to_all x0 -> x1, starting transfers between devices: none -> 12.2 us  [fetch(): lax.all_to_all(jnp.stack([pick_blocks(down_weight, down_mine, offset)] *...]
    all_gather x1, waiting for transfers between devices: 17.8 us -> 27.5 us  [body(): gathered = lax.all_gather(tokens, 'tp', axis=1, tiled=True)]
  transfers between devices with their start and end apart: 7 -> 7, of which waited for: 6 -> 5; matrix products, arithmetic and copies ran while one was open for 24% -> 27% of each run, Pallas kernels for 0% -> 0%
where the time goes in v1:
time: 617 us; the launch traced here: 616 us
  waiting for transfers between devices  295 us (48%)
  other arithmetic  156 us (25%)
  matrix products  68.5 us (11%)
  local copies, waits for them, and re-layouts  68 us (11%)
  between operations  16.4 us (3%)
  starting transfers between devices  12.6 us (2%)
    unnamed x7, waiting for transfers between devices  215 us
    all_to_all x1, waiting for transfers between devices, fetch(): lax.all_to_all(jnp.stack([pick_blocks(down_weight, down_mine, offset)] *...  40.8 us
    scatter-add x1, other arithmetic, body(): jnp.zeros((group_rows, col_blocks, BLK), jnp.float32).at[:, up_table[1], :]  36.7 us
    scatter-add x1, other arithmetic, body(): layer_parts = jnp.zeros((group_rows, row_blocks, BLK), jnp.float32).at[:,...  35.8 us
    scatter-add x1, other arithmetic, body(): jnp.zeros((group_rows, row_blocks, BLK), jnp.float32).at[:, up_table[0], :]  35.7 us
    all_gather x1, waiting for transfers between devices, body(): gathered = lax.all_gather(tokens, 'tp', axis=1, tiled=True)  27.5 us
    scatter-add x1, other arithmetic, body(): jnp.zeros((group_rows, col_blocks, BLK), jnp.float32)  24.4 us
    dot_general x1, matrix products, body(): jnp.einsum('rsk,skn->rsn', dy_taken, down_again, preferred_element_type=j...  13.1 us
  transfers between devices with their start and end apart: 7, of which 5 were waited for; matrix products, arithmetic and copies ran while one was open for 27% of the time, Pallas kernels for 0%

profile of v1, /device:TPU:1, one launch (start us, length us, event | category | flops | bytes accessed | tf_op | source)
XLA Modules:
  0.0 615.8 jit_solution(399774376689263751)
XLA Ops:
  22.9 12.2 %all-to-all-start = ((bf16[32,4,128,128]{3,2,1,0:T(8,128)(2,1)}), bf16[32,4,128,128]{3,2,1,0:T(8,128)(2,1)}, u32[]{:S(2)}, u32[]{:S(2)}) async-start(bf16[32,4,128,128]{3,2,1,0:T(8,128)(2,1)} %stack.11), calls=%async_computation | async-start | bytes 8388608 | tf_op jit(solution)/shard_map/all_to_all | solution.py:79
  38.1 4.4 all-gather.8.cloned.1.call-done
  42.5 3.2 copy.72
  45.7 27.5 %all-gather.6.cloned.1.call-done = bf16[256,4096]{0,1:T(8,128)(2,1)} async-done(((bf16[256,512]{0,1:T(8,128)(2,1)}), bf16[256,4096]{0,1:T(8,128)(2,1)}) %all-gather.6.cloned.1.call-update) | async-done | bytes 2097168 | tf_op jit(solution)/shard_map/all_gather | solution.py:113
  73.2 4.1 copy.65
  77.2 6.5 %gather_fusion.4 = bf16[128,256,128]{2,1,0:T(8,128)(2,1)} fusion(bf16[256,32,128]{2,0,1:T(8,128)(2,1)S(1)} %copy.72, s32[1024]{0:T(1024)S(1)} %pad_clamp_fusion.1), kind=kCustom, calls=%fused_computation.2.clone | custom fusion | bytes 16777728 | tf_op jit(solution)/shard_map/jit(_take)/gather | solution.py:143
  83.7 8.1 %gather_fusion.2 = bf16[128,256,128]{2,1,0:T(8,128)(2,1)} fusion(bf16[256,32,128]{2,0,1:T(8,128)(2,1)} %copy.65, s32[1024]{0:T(1024)S(1)} %pad_clamp_fusion.3), kind=kCustom, calls=%fused_computation.clone | custom fusion | bytes 16777728 | tf_op jit(solution)/shard_map/jit(_take)/gather | solution.py:117
  91.8 40.8 %all-to-all-done = bf16[32,4,128,128]{3,2,1,0:T(8,128)(2,1)} async-done(((bf16[32,4,128,128]{3,2,1,0:T(8,128)(2,1)}), bf16[32,4,128,128]{3,2,1,0:T(8,128)(2,1)}, u32[]{:S(2)}, u32[]{:S(2)}) %all-to-all-start) | async-done | bytes 4194336 | tf_op jit(solution)/shard_map/all_to_all | solution.py:79
  132.7 13.1 %fusion.6 = f32[128,256,128]{2,1,0:T(8,128)} fusion(bf16[128,128,128]{2,1,0:T(8,128)(2,1)} %bitcast.21, bf16[128,256,128]{2,1,0:T(8,128)(2,1)} %gather_fusion.4, pred[128]{0:T(512)(128)(4,1)S(1)} %get-tuple-element.44), kind=kOutput, calls=%fused_computation.19 | convolution fusion | flops 1077936128 | bytes 29360256 | tf_op jit(solution)/shard_map/rsk,skn->rsn/dot_general | solution.py:144
  145.9 24.4 %scatter_fusion.2 = f32[256,14,128]{2,0,1:T(8,128)S(1)} fusion(f32[256,14,128]{2,0,1:T(8,128)S(1)} %broadcast.171.clone, s32[128]{0:T(128)S(1)} %fusion.40, f32[128,256,128]{2,1,0:T(8,128)} %fusion.6), kind=kCustom, calls=%fused_computation.8 | custom fusion | flops 4194304 | bytes 50332160 | tf_op jit(solution)/shard_map/scatter-add | solution.py:146
  170.4 12.7 %fusion.12 = f32[128,256,128]{2,1,0:T(8,128)} fusion(bf16[128,128,128]{2,1,0:T(8,128)(2,1)} %all-gather.4.cloned.1.call-done, bf16[128,256,128]{2,1,0:T(8,128)(2,1)} %gather_fusion.2, pred[128]{0:T(512)(128)(4,1)S(1)} %get-tuple-element.49), kind=kOutput, calls=%fused_computation.25 | convolution fusion | flops 1077936128 | bytes 29360256 | tf_op jit(solution)/shard_map/rsk,skn->rsn/dot_general | solution.py:118
  184.5 36.7 %scatter_fusion = f32[256,14,128]{2,0,1:T(8,128)} fusion(f32[256,14,128]{2,0,1:T(8,128)} %broadcast.171.clone.1, s32[128]{0:T(128)S(1)} %fusion.38, f32[128,256,128]{2,1,0:T(8,128)} %fusion.12), kind=kCustom, calls=%fused_computation.6 | custom fusion | flops 4194304 | bytes 50332160 | tf_op jit(solution)/shard_map/scatter-add | solution.py:120
  221.2 3.7 fusion.28
  225.0 7.7 %gather_fusion.5 = bf16[128,256,128]{2,1,0:T(8,128)(2,1)} fusion(bf16[256,14,128]{2,0,1:T(8,128)(2,1)} %get-tuple-element.36, s32[1024]{0:T(1024)S(1)} %pad_clamp_fusion), kind=kCustom, calls=%fused_computation.3.clone | custom fusion | bytes 16777728 | tf_op jit(solution)/shard_map/jit(_take)/gather | solution.py:149
  232.6 12.7 %fusion.2 = f32[128,256,128]{2,1,0:T(8,128)} fusion(bf16[128,128,128]{2,1,0:T(8,128)(2,1)} %all-gather.4.cloned.1.call-done, bf16[128,256,128]{2,1,0:T(8,128)(2,1)} %gather_fusion.5, pred[128]{0:T(512)(128)(4,1)S(1)} %get-tuple-element.48), kind=kOutput, calls=%fused_computation.15 | convolution fusion | flops 1077936128 | bytes 29360256 | tf_op jit(solution)/shard_map/rsn,skn->rsk/dot_general | solution.py:150
  247.7 35.7 %scatter_fusion.3 = f32[256,32,128]{2,0,1:T(8,128)} fusion(f32[256,32,128]{2,0,1:T(8,128)} %broadcast.165.clone.1, s32[128]{0:T(128)S(1)} %fusion.39, f32[128,256,128]{2,1,0:T(8,128)} %fusion.2), kind=kCustom, calls=%fused_computation.9 | custom fusion | flops 4194304 | bytes 50332160 | tf_op jit(solution)/shard_map/scatter-add | solution.py:152
  288.9 6.7 %gather_fusion.3 = bf16[128,256,128]{2,1,0:T(8,128)(2,1)} fusion(bf16[256,14,128]{2,0,1:T(8,128)(2,1)S(1)} %get-tuple-element.37, s32[1024]{0:T(1024)S(1)} %pad_clamp_fusion.2), kind=kCustom, calls=%fused_computation.1.clone | custom fusion | bytes 16777728 | tf_op jit(solution)/shard_map/jit(_take)/gather | solution.py:123
  295.6 12.7 %fusion.9 = f32[128,256,128]{2,1,0:T(8,128)} fusion(bf16[128,128,128]{2,1,0:T(8,128)(2,1)} %bitcast.21, bf16[128,256,128]{2,1,0:T(8,128)(2,1)} %gather_fusion.3, pred[128]{0:T(512)(128)(4,1)S(1)} %get-tuple-element.45), kind=kOutput, calls=%fused_computation.22 | convolution fusion | flops 1077936128 | bytes 29360256 | tf_op jit(solution)/shard_map/rsn,skn->rsk/dot_general | solution.py:124
  310.9 35.8 %scatter_fusion.1 = f32[256,32,128]{2,0,1:T(8,128)} fusion(f32[256,32,128]{2,0,1:T(8,128)} %broadcast.165.clone, s32[128]{0:T(128)S(1)} %fusion.37, f32[128,256,128]{2,1,0:T(8,128)} %fusion.9), kind=kCustom, calls=%fused_computation.7 | custom fusion | flops 4194304 | bytes 50332160 | tf_op jit(solution)/shard_map/scatter-add | solution.py:130
  352.1 8.1 %convert_bitcast_fusion = bf16[128,1,128,128]{3,2,0,1:T(8,128)(2,1)S(1)} fusion(bf16[128,256,128]{2,1,0:T(8,128)(2,1)} %gather_fusion.3, pred[128]{0:T(512)(128)(4,1)S(1)} %get-tuple-element.45, bf16[128,256,128]{2,1,0:T(8,128)(2,1)} %gather_fusion.4, pred[128]{0:T(512)(128)(4,1)S(1)} %get-tuple-element.44), kind=kOutput, calls=%fused_computation.31 | convolution fusion | flops 1084227584 | bytes 20971776 | tf_op jit(solution)/shard_map/rsk,rsn->skn/dot_general | solution.py:169
  360.2 9.3 %convert_bitcast_fusion.1 = bf16[128,1,128,128]{3,2,0,1:T(8,128)(2,1)} fusion(bf16[128,256,128]{2,1,0:T(8,128)(2,1)} %gather_fusion.5, pred[128]{0:T(512)(128)(4,1)S(1)} %get-tuple-element.48, bf16[128,256,128]{2,1,0:T(8,128)(2,1)} %gather_fusion.2, pred[128]{0:T(512)(128)(4,1)S(1)} %get-tuple-element.49), kind=kOutput, calls=%fused_computation.32 | convolution fusion | flops 1084227584 | bytes 20971776 | tf_op jit(solution)/shard_map/rsk,rsn->skn/dot_general | solution.py:168
  369.5 6.3 %pad_maximum_fusion = bf16[128,2,128,128]{3,2,0,1:T(8,128)(2,1)} fusion(bf16[128,1,128,128]{3,2,0,1:T(8,128)(2,1)S(1)} %convert_bitcast_fusion, bf16[128,1,128,128]{3,2,0,1:T(8,128)(2,1)} %convert_bitcast_fusion.1), kind=kLoop, calls=%fused_computation.12 | loop fusion | flops 4194304 | bytes 16777216 | tf_op jit(solution)/shard_map/stack | solution.py:171
  379.5 7.1 %reduce-scatter.6.cloned.1.call-done = bf16[256,512]{0,1:T(8,128)(2,1)} async-done(((bf16[256,4096]{0,1:T(8,128)(2,1)}), bf16[256,512]{0,1:T(8,128)(2,1)}) %reduce-scatter.6.cloned.1.call-update) | async-done | bytes 262160 | tf_op jit(solution)/shard_map/reduce_scatter | solution.py:132
  388.4 214.7 %all-reduce.3.cloned.1.call-done = bf16[128,2,128,128]{3,2,0,1:T(8,128)(2,1)} async-done(((bf16[128,2,128,128]{3,2,0,1:T(8,128)(2,1)}), bf16[128,2,128,128]{3,2,0,1:T(8,128)(2,1)}) %all-reduce.3.cloned.1.call-update) | async-done | bytes 8388624
  (93 shorter events, 45.4 us)
Async XLA Ops:
  7.2 35.3 %all-gather.8.cloned.1.call-start = ((), (), s32[]{:S(2)}) async-start(), calls=%async_computation.6 | async-start | bytes 2359296 | tf_op jit(solution)/shard_map/all_gather | solution.py:141
  9.0 26.1 %copy-start = (bf16[128,1792]{1,0:T(8,128)(2,1)S(1)}, bf16[128,1792]{1,0:T(8,128)(2,1)}, u32[]{:S(2)}) copy-start(bf16[128,1792]{1,0:T(8,128)(2,1)} %param.14) | copy-start | bytes 1376260
  9.0 64.1 %all-gather.6.cloned.1.call-start = ((), (), s32[]{:S(2)}) async-start(), calls=%async_computation.4 | async-start | bytes 2359296 | tf_op jit(solution)/shard_map/all_gather | solution.py:113
  22.9 109.8 %all-to-all-start = ((bf16[32,4,128,128]{3,2,1,0:T(8,128)(2,1)}), bf16[32,4,128,128]{3,2,1,0:T(8,128)(2,1)}, u32[]{:S(2)}, u32[]{:S(2)}) async-start(bf16[32,4,128,128]{3,2,1,0:T(8,128)(2,1)} %stack.11), calls=%async_computation | async-start | bytes 8388608 | tf_op jit(solution)/shard_map/all_to_all | solution.py:79
  35.1 135.3 %all-gather.4.cloned.1.call-start = ((), (), s32[]{:S(2)}) async-start(), calls=%async_computation.3 | async-start | bytes 4325376 | tf_op jit(solution)/shard_map/all_gather | solution.py:77
  37.7 340.0 %reduce-scatter.8.cloned.1.call-start = ((), (), s32[]{:S(2)}) async-start(), calls=%async_computation.7 | async-start | bytes 2359296 | tf_op jit(solution)/shard_map/reduce_scatter | solution.py:154
  288.8 97.8 %reduce-scatter.6.cloned.1.call-start = ((), (), s32[]{:S(2)}) async-start(), calls=%async_computation.5 | async-start | bytes 2359296 | tf_op jit(solution)/shard_map/reduce_scatter | solution.py:132
  352.1 251.0 %all-reduce.3.cloned.1.call-start = ((), (), s32[]{:S(2)}) async-start(), calls=%async_computation.8 | async-start | bytes 16777216
  375.8 0.7 copy-start.5
  375.8 228.3 %copy-start.1 = (pred[4]{0:T(512)(128)(4,1)S(1)}, pred[4]{0:T(512)(128)(4,1)}, u32[]{:S(2)}) copy-start(pred[4]{0:T(512)(128)(4,1)} %get-tuple-element.28) | copy-start | bytes 16
  375.8 228.3 %copy-start.2 = (pred[4]{0:T(512)(128)(4,1)S(1)}, pred[4]{0:T(512)(128)(4,1)}, u32[]{:S(2)}) copy-start(pred[4]{0:T(512)(128)(4,1)} %get-tuple-element.32) | copy-start | bytes 16
  375.8 228.5 %copy-start.4 = (s32[4]{0:T(128)S(1)}, s32[4]{0:T(128)}, u32[]{:S(2)}) copy-start(s32[4]{0:T(128)} %get-tuple-element.30) | copy-start | bytes 52
  375.8 230.9 %copy-start.3 = (s32[4]{0:T(128)S(1)}, s32[4]{0:T(128)}, u32[]{:S(2)}) copy-start(s32[4]{0:T(128)} %get-tuple-element.46) | copy-start | bytes 52
Sparse Core Ops, SparseCore 0:
  10.4 31.9 all-gather.7
  44.9 28.2 all-gather.5
  76.3 87.5 all-gather.3
  288.9 34.2 reduce-scatter.7
  352.2 34.3 reduce-scatter.5
  390.1 212.8 all-reduce.2
